TPU v7x, 128 devices: a whole 4x4x4 slice. The times are simulated.
128 devices in a mesh: space: 32 (over z, y, core), mode: 4 (over x).
Axes of the slice: x: 4, y: 4, z: 4, core: 2. Of those that a mesh axis runs over, the one named last changes fastest.
Arguments:
- velocity: float32 [3, 512, 512, 256], P(None, 'space', 'mode'), may hold values from -6 to 6
- basis: float32 [32, 3145728], P('mode', 'space'), may hold values from -42 to 42
- levels: float32 [8], replicated, may hold values from 0.02 to 0.15
- profile_index: int32 [256], replicated, may hold values from 0 to 7
- advect: float32 [256], replicated, may hold values from 0 to 0.4
Outputs:
- modes: float32 [32, 3145728], P('mode', 'space')
- sigma: float32 [32], replicated
Inputs may be any that keep to these rules, and one draw needn't show every extreme that they name: `profile_index`: each entry picks one of the 8 viscosity levels.
All inputs are finite; a program needn't handle non-finite values.
Results may differ from a plain program's by a relative error of at most 0.0055.
Values sent between devices are 32-bit elements; how exact they have to be, the bound alone decides.
No kernel may reach another device: no remote copies, remote signals or barrier semaphores. Data moves between devices by JAX's collectives and lax.ppermute only.
A program may use at most 128 MiB of HBM per device.

v0:
```python
import math
import jax
import jax.numpy as jnp
import numpy as np
from jax import lax
from jax.sharding import PartitionSpec as P

STRIDE = 4
MODES = 32
SWEEPS = 2


def extended(x, sides, width):
    for axis, dim in sides:
        size, length = (lax.axis_size(axis), x.shape[dim])
        up = [(i, (i + 1) % size) for i in range(size)]
        down = [(j, i) for i, j in up]
        last = lax.slice_in_dim(x, length - width, length, axis=dim)
        leading = lax.slice_in_dim(x, 0, width, axis=dim)
        before = lax.ppermute(last, axis, up)
        after = lax.ppermute(leading, axis, down)
        x = jnp.concatenate([before, x, after], axis=dim)
    return x


def profile(levels, profile_index):
    table = (
        profile_index[:, None] == jnp.arange(levels.shape[0], dtype=jnp.int32)[None, :]
    ).astype(jnp.float32)
    viscosity = jnp.sum(table * levels[None, :], axis=1)
    middle = 0.5 * (viscosity[:-1] + viscosity[1:])
    face_up = jnp.concatenate([middle, viscosity[-1:]])
    face_down = jnp.concatenate([viscosity[:1], middle])
    return (viscosity, face_down, face_up)


def advance(field, viscosity, face_down, face_up, advect):
    center = field[:, 1:-1, 1:-1, :]
    east = field[:, 2:, 1:-1, :]
    west = field[:, :-2, 1:-1, :]
    north = field[:, 1:-1, 2:, :]
    south = field[:, 1:-1, :-2, :]
    walled = jnp.pad(center, ((0, 0), (0, 0), (0, 0), (1, 1)))
    upward = walled[..., 2:]
    downward = walled[..., :-2]
    lateral = east + west + north + south - 4.0 * center
    vertical = face_up * (upward - center) - face_down * (center - downward)
    return center + viscosity * lateral + vertical - 0.5 * advect * (east - west)


def coarsen(field):
    components, x_cells, z_cells, y_cells = field.shape
    plane = z_cells * y_cells
    slabs = field.reshape(components * (x_cells // STRIDE), STRIDE * plane)
    along_x = slabs[:, 0:plane]
    for offset in range(1, STRIDE):
        along_x = along_x + slabs[:, offset * plane : (offset + 1) * plane]
    lines = along_x.reshape(
        components * (x_cells // STRIDE) * (z_cells // STRIDE), STRIDE * y_cells
    )
    along_z = lines[:, 0:y_cells]
    for offset in range(1, STRIDE):
        along_z = along_z + lines[:, offset * y_cells : (offset + 1) * y_cells]
    cell_ids = jnp.arange(y_cells, dtype=jnp.int32)[:, None] // STRIDE
    box_ids = jnp.arange(y_cells // STRIDE, dtype=jnp.int32)[None, :]
    summing = (cell_ids == box_ids).astype(jnp.float32)
    boxed = jnp.dot(
        along_z, summing, precision=lax.Precision.HIGHEST, preferred_element_type=jnp.float32
    )
    return (boxed / math.sqrt(STRIDE**3)).reshape(-1)


def with_faces(field):
    return extended(field, (("space", 1), ("mode", 2)), 1)


def round_order(count, turn):
    players = [0] + [1 + (i_pos - 1 + turn) % (count - 1) for i_pos in range(1, count)]
    leading = players[: count // 2]
    trailing = [players[count - 1 - k_pos] for k_pos in range(count // 2)]
    return np.array(leading + trailing)


def reorder_table(count, turn):
    current = round_order(count, turn)
    following = round_order(count, (turn + 1) % (count - 1))
    where_now = np.zeros(count, dtype=np.int64)
    where_now[current] = np.arange(count)
    table = np.zeros((count, count), dtype=np.float32)
    table[where_now[following], np.arange(count)] = 1.0
    return table


def jacobi_sweep(joined, tables):
    count = joined.shape[1]
    half = count // 2
    for turn in range(count - 1):
        col_lead = joined[:, :half]
        col_trail = joined[:, half:]
        rot_lead = col_lead[:count]
        rot_trail = col_trail[:count]
        norm_lead = jnp.sum(rot_lead * rot_lead, axis=0)
        norm_trail = jnp.sum(rot_trail * rot_trail, axis=0)
        inner = jnp.sum(rot_lead * rot_trail, axis=0)
        contrast = norm_trail - norm_lead
        orient = jnp.where(contrast >= 0.0, 1.0, -1.0)
        denominator = jnp.abs(contrast) + jnp.sqrt(contrast * contrast + 4.0 * inner * inner)
        positive = denominator > 0.0
        tangent = jnp.where(
            positive, 2.0 * inner * orient / jnp.where(positive, denominator, 1.0), 0.0
        )
        cosine = 1.0 / jnp.sqrt(1.0 + tangent * tangent)
        sine_part = cosine * tangent
        rotated_pairs = jnp.concatenate(
            [cosine * col_lead - sine_part * col_trail, sine_part * col_lead + cosine * col_trail],
            axis=1,
        )
        joined = jnp.dot(
            rotated_pairs,
            tables[turn],
            precision=lax.Precision.HIGHEST,
            preferred_element_type=jnp.float32,
        )
    return joined


def jacobi(upper):
    count = upper.shape[1]
    start_order = round_order(count, 0)
    back_order = np.zeros(count, dtype=np.int64)
    back_order[start_order] = np.arange(count)
    tables = [jnp.asarray(reorder_table(count, turn)) for turn in range(count - 1)]
    joined = jnp.concatenate([upper, jnp.eye(count, dtype=jnp.float32)], axis=0)[:, start_order]
    joined = lax.fori_loop(
        0, SWEEPS, lambda sweep_index, state: jacobi_sweep(state, tables), joined
    )
    joined = joined[:, back_order]
    return (joined[:count], joined[count:])


def row_products(matrix):
    return lax.dot_general(
        matrix,
        matrix,
        (((1,), (1,)), ((), ())),
        precision=lax.Precision.HIGHEST,
        preferred_element_type=jnp.float32,
    )


def per_device(velocity, basis, levels, profile_index, advect):
    viscosity, face_down, face_up = profile(levels, profile_index)
    first = advance(with_faces(velocity), viscosity, face_down, face_up, advect)
    second = advance(with_faces(first), viscosity, face_down, face_up, advect)
    snapshots = jnp.stack([coarsen(first), coarsen(second)])
    own_rows = jnp.concatenate(
        [snapshots, lax.all_to_all(basis, "mode", split_axis=1, concat_axis=0, tiled=True)], axis=0
    )
    gram = row_products(own_rows)
    lower = jnp.linalg.cholesky(lax.psum(gram, ("space", "mode")))
    rotated, right_vecs = jacobi(lower.T)
    kept = rotated[:, :MODES]
    sigma = jnp.sqrt(jnp.sum(kept * kept, axis=0))
    updated = jnp.dot(
        right_vecs[:, :MODES].T,
        own_rows,
        precision=lax.Precision.HIGHEST,
        preferred_element_type=jnp.float32,
    )
    modes = lax.all_to_all(updated, "mode", split_axis=0, concat_axis=1, tiled=True)
    return (modes, sigma)


def solution(mesh):
    return jax.shard_map(
        per_device,
        mesh=mesh,
        in_specs=(P(None, "space", "mode", None), P("mode", "space"), P(), P(), P()),
        out_specs=(P("mode", "space"), P()),
        check_vma=False,
    )
```

profile of v0, /device:TPU:0, one launch (start us, length us, event | category | flops | bytes accessed | tf_op | source)
XLA Modules:
  0.0 329.9 jit_solution(12529537403124820518)
XLA Ops:
  2.7 6.0 %collective-permute-start = (f32[3,1,128,256]{3,2,1,0:T(8,128)}, f32[3,1,128,256]{3,2,1,0:T(8,128)}, u32[]{:S(2)}, u32[]{:S(2)}) collective-permute-start(f32[3,1,128,256]{3,2,1,0:T(8,128)} %get-tuple-element.437), channel_id=1, source_target_pairs={{4,0},{8,4},{12,8},{16,12},{20,16},{24,20},{28,24},{32,28},{36,32}... | collective-permute-start | bytes 1179656 | tf_op jit(solution)/shard_map/ppermute | solution.py:21
  8.8 4.3 %all-to-all-start = ((f32[8,4,24576]{2,0,1:T(8,128)}), f32[8,4,24576]{2,0,1:T(8,128)S(1)}, u32[]{:S(2)}, u32[]{:S(2)}) async-start(f32[8,4,24576]{2,0,1:T(8,128)} %bitcast.223), calls=%async_computation | async-start | bytes 6291456 | tf_op jit(solution)/shard_map/all_to_all | solution.py:157
  17.1 3.9 %constant_dynamic-update-slice_fusion.1 = f32[3,18,128,256]{3,2,1,0:T(8,128)S(1)} fusion(f32[3,18,128,256]{3,2,1,0:T(8,128)S(1)} %constant_dynamic-update-slice_fusion.2, f32[3,16,128,256]{3,2,1,0:T(8,128)} %param.44), kind=kLoop, calls=%fused_computation.1005 | loop fusion | bytes 12582912
  22.1 2.9 copy-done.1
  25.7 3.2 collective-permute-start.2
  29.5 16.9 %collective-permute-done.2 = f32[3,18,1,256]{3,2,1,0:T(1,128)} collective-permute-done((f32[3,18,1,256]{3,2,1,0:T(1,128)}, f32[3,18,1,256]{3,2,1,0:T(1,128)}, u32[]{:S(2)}, u32[]{:S(2)}) %collective-permute-start.2) | collective-permute-done | bytes 55328 | tf_op jit(solution)/shard_map/ppermute | solution.py:21
  47.6 19.5 %fusion.631 = f32[3,16,128,256]{3,2,1,0:T(8,128)S(1)} fusion(f32[3,16,128,256]{3,2,1,0:T(8,128)} %param.44, f32[3,18,128,256]{3,2,1,0:T(8,128)} %copy-done.1, f32[3,18,1,256]{3,2,1,0:T(1,128)} %collective-permute-done.3, f32[3,18,1,256]{3,2,1,0:T(1,128)} %collective-permute-done.2, f32[3,1,128,256]{3,2,1,0:T(8,128)} %collective-permute-done, ...), kind=kLoop, calls=%fused_computation.935 | loop fusion | flops 31457280 | bytes 20561920 | tf_op jit(solution)/shard_map/sub | solution.py:48
  67.1 2.7 copy-done
  70.8 6.2 %reshape.1127 = f32[12,131072]{1,0:T(8,128)} reshape(f32[3,16,128,256]{3,2,1,0:T(8,128)} %copy-done) | data formatting | bytes 12582912 | tf_op jit(solution)/shard_map/reshape | solution.py:54
  78.2 5.2 %slice_add_fusion.3 = f32[12,32768]{1,0:T(8,128)} fusion(f32[12,131072]{1,0:T(8,128)} %reshape.1127), kind=kLoop, calls=%fused_computation.972 | loop fusion | flops 1179648 | bytes 7864320 | tf_op jit(solution)/shard_map/add | solution.py:57
  83.3 2.6 reshape.1128
  86.0 3.0 collective-permute-done.5
  93.0 2.4 convolution_multiply_fusion.1
  98.8 22.4 %fusion.638 = f32[3,16,128,256]{3,2,1,0:T(8,128)} fusion(f32[3,16,128,256]{3,2,1,0:T(8,128)} %copy-done, f32[3,18,1,256]{3,2,1,0:T(1,128)} %collective-permute-done.7, f32[3,1,128,256]{3,2,1,0:T(8,128)S(1)} %collective-permute-done.4, f32[3,1,128,256]{3,2,1,0:T(8,128)} %collective-permute-done.5, f32[3,18,1,256]{3,2,1,0:T(1,128)} %collective-permute-done.6, ...), kind=kLoop, calls=%fused_computation.942 | loop fusion | flops 37748736 | bytes 13484032 | tf_op jit(solution)/shard_map/sub | solution.py:48
  121.2 6.2 %reshape.1129 = f32[12,131072]{1,0:T(8,128)} reshape(f32[3,16,128,256]{3,2,1,0:T(8,128)} %fusion.638) | data formatting | bytes 12582912 | tf_op jit(solution)/shard_map/reshape | solution.py:54
  127.4 5.2 %slice_add_fusion = f32[12,32768]{1,0:T(8,128)} fusion(f32[12,131072]{1,0:T(8,128)} %reshape.1129), kind=kLoop, calls=%fused_computation.969 | loop fusion | flops 1179648 | bytes 7864320 | tf_op jit(solution)/shard_map/add | solution.py:57
  132.6 2.6 reshape.1130
  137.3 3.4 %fusion.651 = f32[34,34]{0,1:T(8,128)S(1)} fusion(f32[32,24576]{1,0:T(8,128)S(1)} %bitcast.219, f32[1,24576]{1,0:T(1,128)S(1)} %stack_reshape.7, f32[1,24576]{1,0:T(1,128)S(1)} %copy-done.2), kind=kOutput, calls=%fused_computation.968 | convolution fusion | flops 342589440 | bytes 3346960 | tf_op jit(solution)/shard_map/dot_general | solution.py:142
  140.8 65.2 %psum.7 = f32[34,34]{0,1:T(8,128)S(1)} all-reduce(f32[34,34]{0,1:T(8,128)S(1)} %fusion.651), channel_id=1, replica_groups=mesh['space'=32,'mode'=4] {'space','mode'}, use_global_device_ids=true, to_apply=%region_1.2 | all-reduce | flops 1156 | bytes 9248 | tf_op jit(solution)/shard_map/psum | solution.py:160
  206.0 3.1 cholesky.20
  212.2 69.3 %while.12 = (s32[]{:T(128)}, f32[68,34]{0,1:T(8,128)S(1)}, s32[]{:T(128)}, f32[17,34]{1,0:T(8,128)S(1)}, f32[17,34]{1,0:T(8,128)}) while((s32[]{:T(128)}, f32[68,34]{0,1:T(8,128)S(1)}, s32[]{:T(128)}, f32[17,34]{1,0:T(8,128)S(1)}, f32[17,34]{1,0:T(8,128)}) %tuple.273), condition=%wide.region_104.105_spmd.clone.clone, body=%wide.region_4.104_spmd.sunk.clone.clone.sunk | while | flops 31557920 | bytes 3821545 | solution.py:134
  282.2 4.7 %convolution_bitcast_fusion = f32[4,8,24576]{2,1,0:T(8,128)} fusion(f32[32,24576]{1,0:T(8,128)S(1)} %bitcast.220, f32[1,24576]{1,0:T(1,128)S(1)} %stack_reshape.7, f32[1,24576]{1,0:T(1,128)S(1)} %copy-done.2, f32[68,34]{0,1:T(8,128)S(1)} %bitcast.224), kind=kOutput, calls=%fused_computation.926 | convolution fusion | flops 322535424 | bytes 6504448 | tf_op jit(solution)/shard_map/dot_general | solution.py:164
  287.0 3.7 %all-to-all-start.1 = ((f32[4,8,24576]{2,1,0:T(8,128)}), f32[4,8,24576]{2,1,0:T(8,128)S(1)}, u32[]{:S(2)}, u32[]{:S(2)}) async-start(f32[4,8,24576]{2,1,0:T(8,128)} %convolution_bitcast_fusion), calls=%async_computation.1 | async-start | bytes 6291456 | tf_op jit(solution)/shard_map/all_to_all | solution.py:170
  291.3 36.9 %all-to-all-done.1 = f32[4,8,24576]{2,1,0:T(8,128)S(1)} async-done(((f32[4,8,24576]{2,1,0:T(8,128)}), f32[4,8,24576]{2,1,0:T(8,128)S(1)}, u32[]{:S(2)}, u32[]{:S(2)}) %all-to-all-start.1) | async-done | bytes 3145760 | tf_op jit(solution)/shard_map/all_to_all | solution.py:170
  (393 shorter events, 94.9 us)
Async XLA Ops:
  0.6 13.7 %copy-start.5 = (s32[34]{0:T(128)S(1)}, s32[34]{0:T(128)}, u32[]{:S(2)}) copy-start(s32[34]{0:T(128)} %constant.168) | copy-start | bytes 412
  0.6 13.1 %copy-start.4 = (f32[8]{0:T(128)S(1)}, f32[8]{0:T(128)}, u32[]{:S(2)}) copy-start(f32[8]{0:T(128)} %param.46) | copy-start | bytes 100
  0.7 13.0 %copy-start.3 = (s32[256]{0:T(256)S(1)}, s32[256]{0:T(256)}, u32[]{:S(2)}) copy-start(s32[256]{0:T(256)} %param.47) | copy-start | bytes 3076
  2.7 14.3 %collective-permute-start.1 = (f32[3,1,128,256]{3,2,1,0:T(8,128)}, f32[3,1,128,256]{3,2,1,0:T(8,128)S(1)}, u32[]{:S(2)}, u32[]{:S(2)}) collective-permute-start(f32[3,1,128,256]{3,2,1,0:T(8,128)} %get-tuple-element.438), channel_id=1, source_target_pairs={{0,4},{4,8},{8,12},{12,16},{16,20},{20,24},{24,28},{28,32},{32,36}... | collective-permute-start | bytes 1179656 | tf_op jit(solution)/shard_map/ppermute | solution.py:20
  2.7 18.3 %collective-permute-start = (f32[3,1,128,256]{3,2,1,0:T(8,128)}, f32[3,1,128,256]{3,2,1,0:T(8,128)}, u32[]{:S(2)}, u32[]{:S(2)}) collective-permute-start(f32[3,1,128,256]{3,2,1,0:T(8,128)} %get-tuple-element.437), channel_id=1, source_target_pairs={{4,0},{8,4},{12,8},{16,12},{20,16},{24,20},{28,24},{32,28},{36,32}... | collective-permute-start | bytes 1179656 | tf_op jit(solution)/shard_map/ppermute | solution.py:21
  8.8 128.5 %all-to-all-start = ((f32[8,4,24576]{2,0,1:T(8,128)}), f32[8,4,24576]{2,0,1:T(8,128)S(1)}, u32[]{:S(2)}, u32[]{:S(2)}) async-start(f32[8,4,24576]{2,0,1:T(8,128)} %bitcast.223), calls=%async_computation | async-start | bytes 6291456 | tf_op jit(solution)/shard_map/all_to_all | solution.py:157
  22.0 2.9 copy-start.1
  25.7 20.7 %collective-permute-start.2 = (f32[3,18,1,256]{3,2,1,0:T(1,128)}, f32[3,18,1,256]{3,2,1,0:T(1,128)}, u32[]{:S(2)}, u32[]{:S(2)}) collective-permute-start(f32[3,18,1,256]{3,2,1,0:T(1,128)} %get-tuple-element.433), channel_id=1, source_target_pairs={{1,0},{2,1},{3,2},{0,3},{5,4},{6,5},{7,6},{4,7},{9,8},{10,9},{11,1... | collective-permute-start | bytes 165896 | tf_op jit(solution)/shard_map/ppermute | solution.py:21
  28.9 18.7 %collective-permute-start.3 = (f32[3,18,1,256]{3,2,1,0:T(1,128)}, f32[3,18,1,256]{3,2,1,0:T(1,128)}, u32[]{:S(2)}, u32[]{:S(2)}) collective-permute-start(f32[3,18,1,256]{3,2,1,0:T(1,128)} %get-tuple-element.434), channel_id=1, source_target_pairs={{0,1},{1,2},{2,3},{3,0},{4,5},{5,6},{6,7},{7,4},{8,9},{9,10},{10,1... | collective-permute-start | bytes 165896 | tf_op jit(solution)/shard_map/ppermute | solution.py:20
  67.1 2.7 copy-start
  76.9 9.0 %collective-permute-start.4 = (f32[3,1,128,256]{3,2,1,0:T(8,128)}, f32[3,1,128,256]{3,2,1,0:T(8,128)S(1)}, u32[]{:S(2)}, u32[]{:S(2)}) collective-permute-start(f32[3,1,128,256]{3,2,1,0:T(8,128)} %get-tuple-element.436), channel_id=1, source_target_pairs={{4,0},{8,4},{12,8},{16,12},{20,16},{24,20},{28,24},{32,28},{36,32}... | collective-permute-start | bytes 1179656 | tf_op jit(solution)/shard_map/ppermute | solution.py:21
  78.2 10.8 %collective-permute-start.5 = (f32[3,1,128,256]{3,2,1,0:T(8,128)}, f32[3,1,128,256]{3,2,1,0:T(8,128)}, u32[]{:S(2)}, u32[]{:S(2)}) collective-permute-start(f32[3,1,128,256]{3,2,1,0:T(8,128)} %get-tuple-element.435), channel_id=1, source_target_pairs={{0,4},{4,8},{8,12},{12,16},{16,20},{20,24},{24,28},{28,32},{32,36}... | collective-permute-start | bytes 1179656 | tf_op jit(solution)/shard_map/ppermute | solution.py:20
  86.0 7.0 %copy-start.8 = (s32[256]{0:T(256)S(1)}, s32[256]{0:T(256)}, u32[]{:S(2)}) copy-start(s32[256]{0:T(256)} %and_select_fusion) | copy-start | bytes 3076
  90.8 7.9 %collective-permute-start.6 = (f32[3,18,1,256]{3,2,1,0:T(1,128)}, f32[3,18,1,256]{3,2,1,0:T(1,128)}, u32[]{:S(2)}, u32[]{:S(2)}) collective-permute-start(f32[3,18,1,256]{3,2,1,0:T(1,128)} %get-tuple-element.431), channel_id=1, source_target_pairs={{1,0},{2,1},{3,2},{0,3},{5,4},{6,5},{7,6},{4,7},{9,8},{10,9},{11,1... | collective-permute-start | bytes 165896 | tf_op jit(solution)/shard_map/ppermute | solution.py:21
  93.0 5.8 %collective-permute-start.7 = (f32[3,18,1,256]{3,2,1,0:T(1,128)}, f32[3,18,1,256]{3,2,1,0:T(1,128)}, u32[]{:S(2)}, u32[]{:S(2)}) collective-permute-start(f32[3,18,1,256]{3,2,1,0:T(1,128)} %get-tuple-element.432), channel_id=1, source_target_pairs={{0,1},{1,2},{2,3},{3,0},{4,5},{5,6},{6,7},{7,4},{8,9},{9,10},{10,1... | collective-permute-start | bytes 165896 | tf_op jit(solution)/shard_map/ppermute | solution.py:20
  127.4 7.8 %copy-start.9 = (s32[256]{0:T(256)S(1)}, s32[256]{0:T(256)}, u32[]{:S(2)}) copy-start(s32[256]{0:T(256)} %and_select_fusion) | copy-start | bytes 3076
  127.4 9.9 %copy-start.2 = (f32[1,24576]{1,0:T(1,128)S(1)}, f32[1,24576]{1,0:T(1,128)}, u32[]{:S(2)}) copy-start(f32[1,24576]{1,0:T(1,128)} %stack_reshape.6) | copy-start | bytes 294916
  132.6 79.6 %copy-start.6 = (f32[17,34]{1,0:T(8,128)S(1)}, f32[17,34]{1,0:T(8,128)}, u32[]{:S(2)}) copy-start(f32[17,34]{1,0:T(8,128)} %constant.970) | copy-start | bytes 6940
  212.2 21.9 %copy-start.7 = (f32[17,34]{1,0:T(8,128)S(1)}, f32[17,34]{1,0:T(8,128)}, u32[]{:S(2)}) copy-start(f32[17,34]{1,0:T(8,128)} %get-tuple-element.801) | copy-start | bytes 6940 | tf_op jit(solution)/shard_map/while
  246.7 22.0 %copy-start.7 = (f32[17,34]{1,0:T(8,128)S(1)}, f32[17,34]{1,0:T(8,128)}, u32[]{:S(2)}) copy-start(f32[17,34]{1,0:T(8,128)} %get-tuple-element.801) | copy-start | bytes 6940 | tf_op jit(solution)/shard_map/while
  287.0 41.3 %all-to-all-start.1 = ((f32[4,8,24576]{2,1,0:T(8,128)}), f32[4,8,24576]{2,1,0:T(8,128)S(1)}, u32[]{:S(2)}, u32[]{:S(2)}) async-start(f32[4,8,24576]{2,1,0:T(8,128)} %convolution_bitcast_fusion), calls=%async_computation.1 | async-start | bytes 6291456 | tf_op jit(solution)/shard_map/all_to_all | solution.py:170
where the time goes:
time: 333 us; the launch traced here: 330 us
  other arithmetic  75.4 us (23%)
  matrix products  68.1 us (20%)
  blocking collectives  65.2 us (20%)
  waiting for transfers between devices  58.1 us (17%)
  local copies, waits for them, and re-layouts  40 us (12%)
  starting transfers between devices  20.6 us (6%)
    psum x1, blocking collectives, per_device(): lower = jnp.linalg.cholesky(lax.psum(gram, ('space', 'mode')))  65.2 us
    dot_general x132, matrix products, jacobi_sweep(): jnp.dot(rotated_pairs, tables[turn], precision=lax.Precision.HIGHEST, pre...  55.7 us
    sub x2, other arithmetic, advance(): center + viscosity * lateral + vertical - 0.5 * advect * (east - west)  42 us
    all_to_all x1, waiting for transfers between devices, per_device(): lax.all_to_all(updated, 'mode', split_axis=0, concat_axis=1, tiled=True)  36.9 us
    ppermute x4, waiting for transfers between devices, extended(): after = lax.ppermute(leading, axis, down)  16.9 us
    ppermute x4, starting transfers between devices, extended(): after = lax.ppermute(leading, axis, down)  12.6 us
    reshape x2, local copies, waits for them, and re-layouts, coarsen(): slabs = field.reshape(components * (x_cells // STRIDE), STRIDE * plane)  12.3 us
    unnamed x21, local copies, waits for them, and re-layouts  11.2 us
  transfers between devices with their start and end apart: 10, of which 4 were waited for; matrix products, arithmetic and copies ran while one was open for 28% of the time, Pallas kernels for 0%

commit v1 on v0

--- a/solution.py
+++ b/solution.py
@@ -157,7 +157,7 @@
         [snapshots, lax.all_to_all(basis, "mode", split_axis=1, concat_axis=0, tiled=True)], axis=0
     )
     gram = row_products(own_rows)
-    lower = jnp.linalg.cholesky(lax.psum(gram, ("space", "mode")))
+    lower = jnp.linalg.cholesky(lax.psum(lax.psum(gram, "mode"), "space"))
     rotated, right_vecs = jacobi(lower.T)
     kept = rotated[:, :MODES]
     sigma = jnp.sqrt(jnp.sum(kept * kept, axis=0))

time: 333 us -> 404 us (1.21)
  blocking collectives: 65.2 us -> 141 us
  waiting for transfers between devices: 58.1 us -> 53.3 us
    psum x1 -> x2, blocking collectives: 65.2 us -> 141 us  [per_device(): lower = jnp.linalg.cholesky(lax.psum(lax.psum(gram, 'mode'), 'space'))]
    all_to_all x1, waiting for transfers between devices: 36.9 us -> 32.2 us  [per_device(): lax.all_to_all(updated, 'mode', split_axis=0, concat_axis=1, tiled=True)]
  transfers between devices with their start and end apart: 10 -> 10, of which waited for: 4 -> 4; matrix products, arithmetic and copies ran while one was open for 28% -> 23% of each run, Pallas kernels for 0% -> 0%
where the time goes in v1:
time: 404 us; the launch traced here: 401 us
  blocking collectives  141 us (35%)
  other arithmetic  75.4 us (19%)
  matrix products  68.1 us (17%)
  waiting for transfers between devices  53.3 us (13%)
  local copies, waits for them, and re-layouts  40 us (10%)
  starting transfers between devices  20.6 us (5%)
    psum x2, blocking collectives, per_device(): lower = jnp.linalg.cholesky(lax.psum(lax.psum(gram, 'mode'), 'space'))  141 us
    dot_general x132, matrix products, jacobi_sweep(): jnp.dot(rotated_pairs, tables[turn], precision=lax.Precision.HIGHEST, pre...  55.7 us
    sub x2, other arithmetic, advance(): center + viscosity * lateral + vertical - 0.5 * advect * (east - west)  42 us
    all_to_all x1, waiting for transfers between devices, per_device(): lax.all_to_all(updated, 'mode', split_axis=0, concat_axis=1, tiled=True)  32.2 us
    ppermute x4, waiting for transfers between devices, extended(): after = lax.ppermute(leading, axis, down)  16.9 us
    ppermute x4, starting transfers between devices, extended(): after = lax.ppermute(leading, axis, down)  12.6 us
    reshape x2, local copies, waits for them, and re-layouts, coarsen(): slabs = field.reshape(components * (x_cells // STRIDE), STRIDE * plane)  12.3 us
    unnamed x21, local copies, waits for them, and re-layouts  11.2 us
  transfers between devices with their start and end apart: 10, of which 4 were waited for; matrix products, arithmetic and copies ran while one was open for 23% of the time, Pallas kernels for 0%

profile of v1, /device:TPU:0, one launch (start us, length us, event | category | flops | bytes accessed | tf_op | source)
XLA Modules:
  0.0 401.5 jit_solution(7749393859909539071)
XLA Ops:
  2.7 6.0 %collective-permute-start = (f32[3,1,128,256]{3,2,1,0:T(8,128)}, f32[3,1,128,256]{3,2,1,0:T(8,128)}, u32[]{:S(2)}, u32[]{:S(2)}) collective-permute-start(f32[3,1,128,256]{3,2,1,0:T(8,128)} %get-tuple-element.437), channel_id=1, source_target_pairs={{4,0},{8,4},{12,8},{16,12},{20,16},{24,20},{28,24},{32,28},{36,32}... | collective-permute-start | bytes 1179656 | tf_op jit(solution)/shard_map/ppermute | solution.py:21
  8.8 4.3 %all-to-all-start = ((f32[8,4,24576]{2,0,1:T(8,128)}), f32[8,4,24576]{2,0,1:T(8,128)S(1)}, u32[]{:S(2)}, u32[]{:S(2)}) async-start(f32[8,4,24576]{2,0,1:T(8,128)} %bitcast.223), calls=%async_computation | async-start | bytes 6291456 | tf_op jit(solution)/shard_map/all_to_all | solution.py:157
  17.1 3.9 constant_dynamic-update-slice_fusion.1
  22.1 2.9 copy-done.1
  25.7 3.2 collective-permute-start.2
  29.5 16.9 %collective-permute-done.2 = f32[3,18,1,256]{3,2,1,0:T(1,128)} collective-permute-done((f32[3,18,1,256]{3,2,1,0:T(1,128)}, f32[3,18,1,256]{3,2,1,0:T(1,128)}, u32[]{:S(2)}, u32[]{:S(2)}) %collective-permute-start.2) | collective-permute-done | bytes 55328 | tf_op jit(solution)/shard_map/ppermute | solution.py:21
  47.6 19.5 %fusion.631 = f32[3,16,128,256]{3,2,1,0:T(8,128)S(1)} fusion(f32[3,16,128,256]{3,2,1,0:T(8,128)} %param.44, f32[3,18,128,256]{3,2,1,0:T(8,128)} %copy-done.1, f32[3,18,1,256]{3,2,1,0:T(1,128)} %collective-permute-done.3, f32[3,18,1,256]{3,2,1,0:T(1,128)} %collective-permute-done.2, f32[3,1,128,256]{3,2,1,0:T(8,128)} %collective-permute-done, ...), kind=kLoop, calls=%fused_computation.935 | loop fusion | flops 31457280 | bytes 20561920 | tf_op jit(solution)/shard_map/sub | solution.py:48
  67.1 2.7 copy-done
  70.8 6.2 %reshape.1127 = f32[12,131072]{1,0:T(8,128)} reshape(f32[3,16,128,256]{3,2,1,0:T(8,128)} %copy-done) | data formatting | bytes 12582912 | tf_op jit(solution)/shard_map/reshape | solution.py:54
  78.2 5.2 %slice_add_fusion.3 = f32[12,32768]{1,0:T(8,128)} fusion(f32[12,131072]{1,0:T(8,128)} %reshape.1127), kind=kLoop, calls=%fused_computation.972 | loop fusion | flops 1179648 | bytes 7864320 | tf_op jit(solution)/shard_map/add | solution.py:57
  83.3 2.6 reshape.1128
  86.0 3.0 collective-permute-done.5
  98.8 22.4 %fusion.638 = f32[3,16,128,256]{3,2,1,0:T(8,128)} fusion(f32[3,16,128,256]{3,2,1,0:T(8,128)} %copy-done, f32[3,18,1,256]{3,2,1,0:T(1,128)} %collective-permute-done.7, f32[3,1,128,256]{3,2,1,0:T(8,128)S(1)} %collective-permute-done.4, f32[3,1,128,256]{3,2,1,0:T(8,128)} %collective-permute-done.5, f32[3,18,1,256]{3,2,1,0:T(1,128)} %collective-permute-done.6, ...), kind=kLoop, calls=%fused_computation.942 | loop fusion | flops 37748736 | bytes 13484032 | tf_op jit(solution)/shard_map/sub | solution.py:48
  121.2 6.2 %reshape.1129 = f32[12,131072]{1,0:T(8,128)} reshape(f32[3,16,128,256]{3,2,1,0:T(8,128)} %fusion.638) | data formatting | bytes 12582912 | tf_op jit(solution)/shard_map/reshape | solution.py:54
  127.4 5.2 %slice_add_fusion = f32[12,32768]{1,0:T(8,128)} fusion(f32[12,131072]{1,0:T(8,128)} %reshape.1129), kind=kLoop, calls=%fused_computation.969 | loop fusion | flops 1179648 | bytes 7864320 | tf_op jit(solution)/shard_map/add | solution.py:57
  132.6 2.6 reshape.1130
  137.3 3.4 fusion.651
  140.8 17.5 %psum.14 = f32[34,34]{0,1:T(8,128)S(1)} all-reduce(f32[34,34]{0,1:T(8,128)S(1)} %fusion.651), channel_id=1, replica_groups=mesh['space'=32,'mode'=4] {'mode'}, use_global_device_ids=true, to_apply=%region_1.2 | all-reduce | flops 1156 | bytes 9248 | tf_op jit(solution)/shard_map/psum | solution.py:160
  158.2 124.0 %psum.15 = f32[34,34]{0,1:T(8,128)S(1)} all-reduce(f32[34,34]{0,1:T(8,128)S(1)} %psum.14), channel_id=1, replica_groups=mesh['space'=32,'mode'=4] {'space'}, use_global_device_ids=true, to_apply=%region_2.3 | all-reduce | flops 1156 | bytes 9248 | tf_op jit(solution)/shard_map/psum | solution.py:160
  282.3 3.1 cholesky.20
  288.5 69.3 %while.12 = (s32[]{:T(128)}, f32[68,34]{0,1:T(8,128)S(1)}, s32[]{:T(128)}, f32[17,34]{1,0:T(8,128)S(1)}, f32[17,34]{1,0:T(8,128)}) while((s32[]{:T(128)}, f32[68,34]{0,1:T(8,128)S(1)}, s32[]{:T(128)}, f32[17,34]{1,0:T(8,128)S(1)}, f32[17,34]{1,0:T(8,128)}) %tuple.273), condition=%wide.region_105.106_spmd.clone.clone, body=%wide.region_5.105_spmd.sunk.clone.clone.sunk | while | flops 31557920 | bytes 3821545 | solution.py:134
  358.5 4.7 %convolution_bitcast_fusion = f32[4,8,24576]{2,1,0:T(8,128)} fusion(f32[32,24576]{1,0:T(8,128)S(1)} %bitcast.220, f32[1,24576]{1,0:T(1,128)S(1)} %stack_reshape.7, f32[1,24576]{1,0:T(1,128)S(1)} %copy-done.2, f32[68,34]{0,1:T(8,128)S(1)} %bitcast.224), kind=kOutput, calls=%fused_computation.926 | convolution fusion | flops 322535424 | bytes 6504448 | tf_op jit(solution)/shard_map/dot_general | solution.py:164
  363.3 3.7 all-to-all-start.1
  367.6 32.2 %all-to-all-done.1 = f32[4,8,24576]{2,1,0:T(8,128)S(1)} async-done(((f32[4,8,24576]{2,1,0:T(8,128)}), f32[4,8,24576]{2,1,0:T(8,128)S(1)}, u32[]{:S(2)}, u32[]{:S(2)}) %all-to-all-start.1) | async-done | bytes 3145760 | tf_op jit(solution)/shard_map/all_to_all | solution.py:170
  (394 shorter events, 97.4 us)
Async XLA Ops:
  0.6 13.7 %copy-start.5 = (s32[34]{0:T(128)S(1)}, s32[34]{0:T(128)}, u32[]{:S(2)}) copy-start(s32[34]{0:T(128)} %constant.168) | copy-start | bytes 412
  0.6 13.1 %copy-start.4 = (f32[8]{0:T(128)S(1)}, f32[8]{0:T(128)}, u32[]{:S(2)}) copy-start(f32[8]{0:T(128)} %param.46) | copy-start | bytes 100
  0.7 13.0 %copy-start.3 = (s32[256]{0:T(256)S(1)}, s32[256]{0:T(256)}, u32[]{:S(2)}) copy-start(s32[256]{0:T(256)} %param.47) | copy-start | bytes 3076
  2.7 14.3 %collective-permute-start.1 = (f32[3,1,128,256]{3,2,1,0:T(8,128)}, f32[3,1,128,256]{3,2,1,0:T(8,128)S(1)}, u32[]{:S(2)}, u32[]{:S(2)}) collective-permute-start(f32[3,1,128,256]{3,2,1,0:T(8,128)} %get-tuple-element.438), channel_id=1, source_target_pairs={{0,4},{4,8},{8,12},{12,16},{16,20},{20,24},{24,28},{28,32},{32,36}... | collective-permute-start | bytes 1179656 | tf_op jit(solution)/shard_map/ppermute | solution.py:20
  2.7 18.3 %collective-permute-start = (f32[3,1,128,256]{3,2,1,0:T(8,128)}, f32[3,1,128,256]{3,2,1,0:T(8,128)}, u32[]{:S(2)}, u32[]{:S(2)}) collective-permute-start(f32[3,1,128,256]{3,2,1,0:T(8,128)} %get-tuple-element.437), channel_id=1, source_target_pairs={{4,0},{8,4},{12,8},{16,12},{20,16},{24,20},{28,24},{32,28},{36,32}... | collective-permute-start | bytes 1179656 | tf_op jit(solution)/shard_map/ppermute | solution.py:21
  8.8 128.5 %all-to-all-start = ((f32[8,4,24576]{2,0,1:T(8,128)}), f32[8,4,24576]{2,0,1:T(8,128)S(1)}, u32[]{:S(2)}, u32[]{:S(2)}) async-start(f32[8,4,24576]{2,0,1:T(8,128)} %bitcast.223), calls=%async_computation | async-start | bytes 6291456 | tf_op jit(solution)/shard_map/all_to_all | solution.py:157
  22.0 2.9 copy-start.1
  25.7 20.7 %collective-permute-start.2 = (f32[3,18,1,256]{3,2,1,0:T(1,128)}, f32[3,18,1,256]{3,2,1,0:T(1,128)}, u32[]{:S(2)}, u32[]{:S(2)}) collective-permute-start(f32[3,18,1,256]{3,2,1,0:T(1,128)} %get-tuple-element.433), channel_id=1, source_target_pairs={{1,0},{2,1},{3,2},{0,3},{5,4},{6,5},{7,6},{4,7},{9,8},{10,9},{11,1... | collective-permute-start | bytes 165896 | tf_op jit(solution)/shard_map/ppermute | solution.py:21
  28.9 18.7 %collective-permute-start.3 = (f32[3,18,1,256]{3,2,1,0:T(1,128)}, f32[3,18,1,256]{3,2,1,0:T(1,128)}, u32[]{:S(2)}, u32[]{:S(2)}) collective-permute-start(f32[3,18,1,256]{3,2,1,0:T(1,128)} %get-tuple-element.434), channel_id=1, source_target_pairs={{0,1},{1,2},{2,3},{3,0},{4,5},{5,6},{6,7},{7,4},{8,9},{9,10},{10,1... | collective-permute-start | bytes 165896 | tf_op jit(solution)/shard_map/ppermute | solution.py:20
  67.1 2.7 copy-start
  76.9 9.0 %collective-permute-start.4 = (f32[3,1,128,256]{3,2,1,0:T(8,128)}, f32[3,1,128,256]{3,2,1,0:T(8,128)S(1)}, u32[]{:S(2)}, u32[]{:S(2)}) collective-permute-start(f32[3,1,128,256]{3,2,1,0:T(8,128)} %get-tuple-element.436), channel_id=1, source_target_pairs={{4,0},{8,4},{12,8},{16,12},{20,16},{24,20},{28,24},{32,28},{36,32}... | collective-permute-start | bytes 1179656 | tf_op jit(solution)/shard_map/ppermute | solution.py:21
  78.2 10.8 %collective-permute-start.5 = (f32[3,1,128,256]{3,2,1,0:T(8,128)}, f32[3,1,128,256]{3,2,1,0:T(8,128)}, u32[]{:S(2)}, u32[]{:S(2)}) collective-permute-start(f32[3,1,128,256]{3,2,1,0:T(8,128)} %get-tuple-element.435), channel_id=1, source_target_pairs={{0,4},{4,8},{8,12},{12,16},{16,20},{20,24},{24,28},{28,32},{32,36}... | collective-permute-start | bytes 1179656 | tf_op jit(solution)/shard_map/ppermute | solution.py:20
  86.0 7.0 %copy-start.8 = (s32[256]{0:T(256)S(1)}, s32[256]{0:T(256)}, u32[]{:S(2)}) copy-start(s32[256]{0:T(256)} %and_select_fusion) | copy-start | bytes 3076
  90.8 7.9 %collective-permute-start.6 = (f32[3,18,1,256]{3,2,1,0:T(1,128)}, f32[3,18,1,256]{3,2,1,0:T(1,128)}, u32[]{:S(2)}, u32[]{:S(2)}) collective-permute-start(f32[3,18,1,256]{3,2,1,0:T(1,128)} %get-tuple-element.431), channel_id=1, source_target_pairs={{1,0},{2,1},{3,2},{0,3},{5,4},{6,5},{7,6},{4,7},{9,8},{10,9},{11,1... | collective-permute-start | bytes 165896 | tf_op jit(solution)/shard_map/ppermute | solution.py:21
  93.0 5.8 %collective-permute-start.7 = (f32[3,18,1,256]{3,2,1,0:T(1,128)}, f32[3,18,1,256]{3,2,1,0:T(1,128)}, u32[]{:S(2)}, u32[]{:S(2)}) collective-permute-start(f32[3,18,1,256]{3,2,1,0:T(1,128)} %get-tuple-element.432), channel_id=1, source_target_pairs={{0,1},{1,2},{2,3},{3,0},{4,5},{5,6},{6,7},{7,4},{8,9},{9,10},{10,1... | collective-permute-start | bytes 165896 | tf_op jit(solution)/shard_map/ppermute | solution.py:20
  127.4 7.8 %copy-start.9 = (s32[256]{0:T(256)S(1)}, s32[256]{0:T(256)}, u32[]{:S(2)}) copy-start(s32[256]{0:T(256)} %and_select_fusion) | copy-start | bytes 3076
  127.4 9.9 %copy-start.2 = (f32[1,24576]{1,0:T(1,128)S(1)}, f32[1,24576]{1,0:T(1,128)}, u32[]{:S(2)}) copy-start(f32[1,24576]{1,0:T(1,128)} %stack_reshape.6) | copy-start | bytes 294916
  132.6 155.9 %copy-start.6 = (f32[17,34]{1,0:T(8,128)S(1)}, f32[17,34]{1,0:T(8,128)}, u32[]{:S(2)}) copy-start(f32[17,34]{1,0:T(8,128)} %constant.970) | copy-start | bytes 6940
  288.5 21.9 %copy-start.7 = (f32[17,34]{1,0:T(8,128)S(1)}, f32[17,34]{1,0:T(8,128)}, u32[]{:S(2)}) copy-start(f32[17,34]{1,0:T(8,128)} %get-tuple-element.801) | copy-start | bytes 6940 | tf_op jit(solution)/shard_map/while
  323.0 22.0 %copy-start.7 = (f32[17,34]{1,0:T(8,128)S(1)}, f32[17,34]{1,0:T(8,128)}, u32[]{:S(2)}) copy-start(f32[17,34]{1,0:T(8,128)} %get-tuple-element.801) | copy-start | bytes 6940 | tf_op jit(solution)/shard_map/while
  363.3 36.5 %all-to-all-start.1 = ((f32[4,8,24576]{2,1,0:T(8,128)}), f32[4,8,24576]{2,1,0:T(8,128)S(1)}, u32[]{:S(2)}, u32[]{:S(2)}) async-start(f32[4,8,24576]{2,1,0:T(8,128)} %convolution_bitcast_fusion), calls=%async_computation.1 | async-start | bytes 6291456 | tf_op jit(solution)/shard_map/all_to_all | solution.py:170
